TPU v7x, 32 devices: a whole 2x2x4 slice. The times are simulated.
32 devices in a mesh: ctx: 8 (over z, x), head: 4 (over y, core).
Axes of the slice: x: 2, y: 2, z: 4, core: 2. Of those that a mesh axis runs over, the one named last changes fastest.
Arguments:
- queries: bfloat16 [1024, 8192], P('ctx', 'head'), may hold values from -110 to 110
- key_heads: bfloat16 [1024, 1024], P('ctx'), may hold values from -4.61 to 4.61
- value_heads: bfloat16 [1024, 1024], P('ctx'), may hold values from -6 to 6
- span_order: int32 [16], replicated, may hold values from 0 to 15, each once
- block_mask: int32 [16, 16], replicated, may hold values 0 or 1
- mamba_in: bfloat16 [1024, 16384], P('ctx', 'head'), may hold values from -6 to 6
- gate_in: bfloat16 [1024, 16384], P('ctx', 'head'), may hold values from -6 to 6
- conv_weight: float32 [4, 16384], P(None, 'head'), may hold values from -3 to 3
- conv_bias: float32 [16384], P('head'), may hold values from -3 to 3
- low_weight: bfloat16 [16384, 512], P('head'), may hold values from -0.046875 to 0.046875
- bc_weight: bfloat16 [16384, 32], P('head'), may hold values from -0.046875 to 0.046875
- low_gain: float32 [512], replicated, may hold values from 0.1 to 1.9
- dt_weight: bfloat16 [512, 16384], P(None, 'head'), may hold values from -0.25 to 0.25
- dt_bias: float32 [16384], P('head'), may hold values from -7 to -2
- rate_log: float32 [16384, 16], P('head'), may hold values from -3 to 2.77
- skip_gain: float32 [16384], P('head'), may hold values from 0.5 to 1.5
Outputs:
- attn_out: bfloat16 [1024, 8192], P('ctx', 'head')
- mamba_out: bfloat16 [1024, 16384], P('ctx', 'head')
Inputs may be any that keep to these rules, and one draw needn't show every extreme that they name: `span_order`: each of the 16 span numbers stands in exactly one slot.
All inputs are finite; a program needn't handle non-finite values.
Results may differ from a plain program's by a relative error of at most 0.013.
Values may be sent and summed in bfloat16 or wider, within the bound.
No kernel may reach another device: no remote copies, remote signals or barrier semaphores. Data moves between devices by JAX's collectives and lax.ppermute only.
A program may use at most 192 MiB of HBM per device.

v0:
```python
import math
import jax
import jax.numpy as jnp
from jax import lax
from jax.sharding import PartitionSpec as P

HD = 128
STATE = 16
CONV = 4
NEG_FILL = -1e30


def prefix(shard, axis, join, neutral):
    place = lax.axis_index(axis)
    gathered = jax.tree.map(
        lambda a, kind: lax.all_gather(a.astype(kind), axis), shard, (jnp.bfloat16, jnp.bfloat16)
    )
    state = jax.tree.map(lambda a, e: jnp.zeros_like(a) + jnp.asarray(e, a.dtype), shard, neutral)

    def one(turn, state):
        return join(
            state,
            jax.tree.map(
                lambda a, own: lax.dynamic_index_in_dim(a, turn, 0, False).astype(own.dtype),
                gathered,
                shard,
            ),
        )

    return lax.fori_loop(0, place, one, state)


def passed_along(value, axis, steps):
    count = lax.axis_size(axis)
    first, last = (max(0, -steps), min(count, count - steps))
    return lax.ppermute(value, axis, [(source, source + steps) for source in range(first, last)])


def table_lookup(lookup_table, wanted):
    entries = lookup_table.shape[0]
    matches = wanted[:, None] == jnp.arange(entries, dtype=jnp.int32)[None, :]
    return jnp.sum(jnp.where(matches, lookup_table[None, :], 0), axis=1)


def attend(state, piece, context):
    queries4, query_pos, query_half, own_spans, mask_rows, span_order, half_rows = context
    key_piece, value_piece = piece
    piece_rows = key_piece.shape[0]
    row_ids = jnp.arange(piece_rows, dtype=jnp.int32)
    key_span = table_lookup(span_order, row_ids // half_rows)
    key_pos = key_span * half_rows + row_ids % half_rows
    entries = span_order.shape[0]
    picked = key_span[None, :, None] == jnp.arange(entries, dtype=jnp.int32)[None, None, :]
    granted = jnp.sum(jnp.where(picked, mask_rows[:, None, :], 0), axis=2)
    allowed = (granted == 1) | (key_span[None, :] == own_spans[:, None])
    allowed_rows = jnp.where(query_half[:, None] == 0, allowed[0][None, :], allowed[1][None, :])
    visible = allowed_rows & (key_pos[None, :] <= query_pos[:, None])
    local_kv = queries4.shape[1]
    key_split = key_piece.reshape(piece_rows, local_kv, HD)
    value_split = value_piece.reshape(piece_rows, local_kv, HD)
    scores = jnp.einsum(
        "rkgd,mkd->kgrm", queries4, key_split, preferred_element_type=jnp.float32
    ) * HD ** (-0.5)
    scores = jnp.where(visible[None, None], scores, NEG_FILL)
    running, totals, summed = state
    highest = jnp.maximum(running, jnp.max(scores, axis=3))
    weights = jnp.where(visible[None, None], jnp.exp(scores - highest[..., None]), 0.0)
    totals = jnp.sum(weights, axis=3)
    summed = jnp.einsum(
        "kgrm,mkd->kgrd",
        weights.astype(jnp.bfloat16),
        value_split,
        preferred_element_type=jnp.float32,
    )
    return (highest, totals, summed)


def attention(queries, key_heads, value_heads, span_order, block_mask):
    row_count = queries.shape[0]
    half_rows = row_count // 2
    head_devices = lax.axis_size("head")
    kv_count = key_heads.shape[1] // HD
    local_kv = max(1, kv_count // head_devices)
    query_local = queries.shape[1] // HD
    per_group = query_local // local_kv
    group_size = query_local * head_devices // kv_count
    kv_start = lax.axis_index("head") * query_local // group_size
    key_mine = lax.dynamic_slice_in_dim(key_heads, kv_start * HD, local_kv * HD, 1)
    value_mine = lax.dynamic_slice_in_dim(value_heads, kv_start * HD, local_kv * HD, 1)
    queries4 = queries.reshape(row_count, local_kv, per_group, HD)
    own_slot = lax.axis_index("ctx")
    own_spans = lax.dynamic_slice_in_dim(span_order, 2 * own_slot, 2)
    entries = span_order.shape[0]
    chosen = own_spans[:, None] == jnp.arange(entries, dtype=jnp.int32)[None, :]
    mask_rows = jnp.sum(jnp.where(chosen[:, :, None], block_mask[None], 0), axis=1)
    row_ids = jnp.arange(row_count, dtype=jnp.int32)
    query_half = row_ids // half_rows
    query_span = jnp.where(query_half == 0, own_spans[0], own_spans[1])
    query_pos = query_span * half_rows + row_ids % half_rows
    context = (queries4, query_pos, query_half, own_spans, mask_rows, span_order, half_rows)
    start_state = (
        jnp.full((local_kv, per_group, row_count), NEG_FILL, jnp.float32),
        jnp.zeros((local_kv, per_group, row_count), jnp.float32),
        jnp.zeros((local_kv, per_group, row_count, HD), jnp.float32),
    )
    highest, totals, summed = attend(
        start_state,
        (
            lax.all_gather(key_mine, "ctx", axis=0, tiled=True),
            lax.all_gather(value_mine, "ctx", axis=0, tiled=True),
        ),
        context,
    )
    result = summed / totals[..., None]
    return result.transpose(2, 0, 1, 3).reshape(row_count, -1).astype(jnp.bfloat16)


def link(earlier, later):
    return (earlier[0] * later[0], earlier[1] * later[0] + later[1])


def local_scan(step_dt, inputs_f, b_vals, c_vals, rate_table, carry_in, length):
    row_count, channels = step_dt.shape
    blocks = row_count // length
    decay_all = jnp.exp(step_dt[:, None, :] * rate_table[None])
    drive_all = (step_dt * inputs_f)[:, None, :] * b_vals[:, :, None]

    def one_block(state, packed):
        decay_block, drive_block, c_block = packed
        results = []
        for offset in range(length):
            state = decay_block[offset] * state + drive_block[offset]
            results.append(jnp.sum(state * c_block[offset][:, None], axis=0))
        return (state, jnp.stack(results, axis=0))

    packed = (
        decay_all.reshape(blocks, length, STATE, channels),
        drive_all.reshape(blocks, length, STATE, channels),
        c_vals.reshape(blocks, length, STATE),
    )
    last_state, outputs = lax.scan(one_block, carry_in, packed)
    return (last_state, outputs.reshape(row_count, channels))


def carry_across(through, own_end):
    return prefix(
        (through, own_end), "ctx", link, (jnp.ones_like(through), jnp.zeros_like(own_end))
    )[1]


def normalize(low_vals, low_gain):
    scale_inv = lax.rsqrt(jnp.mean(low_vals * low_vals, axis=1, keepdims=True) + 1e-06)
    return (low_vals * scale_inv * low_gain[None, :]).astype(jnp.bfloat16)


def mamba(
    mamba_in,
    gate_in,
    conv_weight,
    conv_bias,
    low_weight,
    bc_weight,
    low_gain,
    dt_weight,
    dt_bias,
    rate_log,
    skip_gain,
):
    row_count, channels = mamba_in.shape
    rim = passed_along(mamba_in[row_count - (CONV - 1) :], "ctx", 1)
    extended = jnp.concatenate([rim, mamba_in], axis=0)
    mixed = conv_bias[None, :] + sum(
        (
            conv_weight[offset][None, :] * extended[offset : offset + row_count].astype(jnp.float32)
            for offset in range(CONV)
        )
    )
    act_bf = jax.nn.silu(mixed).astype(jnp.bfloat16)
    low_part = jnp.dot(act_bf, low_weight, preferred_element_type=jnp.float32)
    bc_part = jnp.dot(act_bf, bc_weight, preferred_element_type=jnp.float32)
    low_sum, bc_sum = (
        lax.psum(low_part.astype(jnp.bfloat16), "head").astype(jnp.float32),
        lax.psum(bc_part.astype(jnp.bfloat16), "head").astype(jnp.float32),
    )
    normed = normalize(low_sum, low_gain)
    step_dt = jax.nn.softplus(
        jnp.dot(normed, dt_weight, preferred_element_type=jnp.float32) + dt_bias[None, :]
    )
    rate_table = -jnp.exp(rate_log).T
    inputs_f = act_bf.astype(jnp.float32)
    b_vals = bc_sum[:, :STATE]
    c_vals = bc_sum[:, STATE:]
    length = math.gcd(row_count, 32)
    empty = jnp.zeros((STATE, channels), jnp.float32)
    through = jnp.exp(rate_table * jnp.sum(step_dt, axis=0)[None, :])
    own_end = local_scan(step_dt, inputs_f, b_vals, c_vals, rate_table, empty, length)[0]
    entering = carry_across(through, own_end)
    outputs = local_scan(step_dt, inputs_f, b_vals, c_vals, rate_table, entering, length)[1]
    result = outputs + skip_gain[None, :] * inputs_f
    return (result * jax.nn.silu(gate_in.astype(jnp.float32))).astype(jnp.bfloat16)


def per_device(
    queries,
    key_heads,
    value_heads,
    span_order,
    block_mask,
    mamba_in,
    gate_in,
    conv_weight,
    conv_bias,
    low_weight,
    bc_weight,
    low_gain,
    dt_weight,
    dt_bias,
    rate_log,
    skip_gain,
):
    attn_out = attention(queries, key_heads, value_heads, span_order, block_mask)
    mamba_out = mamba(
        mamba_in,
        gate_in,
        conv_weight,
        conv_bias,
        low_weight,
        bc_weight,
        low_gain,
        dt_weight,
        dt_bias,
        rate_log,
        skip_gain,
    )
    return (attn_out, mamba_out)


def solution(mesh):
    in_specs = (
        P("ctx", "head"),
        P("ctx", None),
        P("ctx", None),
        P(),
        P(),
        P("ctx", "head"),
        P("ctx", "head"),
        P(None, "head"),
        P("head"),
        P("head", None),
        P("head", None),
        P(),
        P(None, "head"),
        P("head"),
        P("head", None),
        P("head"),
    )
    out_specs = (P("ctx", "head"), P("ctx", "head"))
    return jax.shard_map(
        per_device, mesh=mesh, in_specs=in_specs, out_specs=out_specs, check_vma=False
    )
```

profile of v0, /device:TPU:26, one launch (start us, length us, event | category | flops | bytes accessed | tf_op | source)
XLA Modules:
  0.0 294.0 jit_solution(15363560117941585995)
XLA Ops:
  8.1 1.3 collective-permute-start
  15.6 3.5 %multiply_convert_fusion = bf16[128,4096]{1,0:T(8,128)(2,1)S(1)} fusion(bf16[128,4096]{1,0:T(8,128)(2,1)} %param.27, bf16[3,4096]{1,0:T(4,128)(2,1)S(1)} %collective-permute-done, f32[4096]{0:T(1024)S(1)} %bitcast.1187, f32[4096]{0:T(1024)S(1)} %bitcast.1188, f32[4096]{0:T(1024)S(1)} %bitcast.1186, f32[4096]{0:T(1024)S(1)} %bitcast.1185, f32[4096]{0:T(1024)} %param.30), kind=kLoop, calls=%fused_computation.376 | loop fusion | flops 13631488 | bytes 2203648 | tf_op jit(solution)/shard_map/convert_element_type | solution.py:178
  19.2 4.0 %convolution_convert_fusion = bf16[128,512]{1,0:T(8,128)(2,1)} fusion(bf16[128,4096]{1,0:T(8,128)(2,1)S(1)} %multiply_convert_fusion, bf16[4096,512]{1,0:T(8,128)(2,1)} %param.31), kind=kOutput, calls=%fused_computation.380 | convolution fusion | flops 536936448 | bytes 5373952 | tf_op jit(solution)/shard_map/dot_general | solution.py:179
  23.6 7.1 %psum.15 = bf16[128,32]{0,1:T(8,128)(2,1)S(1)} all-reduce(bf16[128,32]{0,1:T(8,128)(2,1)S(1)} %convolution_convert_fusion.1), channel_id=1, replica_groups=mesh['ctx'=8,'head'=4] {'head'}, use_global_device_ids=true, to_apply=%region_8.9 | all-reduce | flops 4096 | bytes 16384 | tf_op jit(solution)/shard_map/psum | solution.py:183
  30.9 26.4 %all-reduce.2.cloned.1.call-done = bf16[128,512]{1,0:T(8,128)(2,1)} async-done(((bf16[128,512]{1,0:T(8,128)(2,1)}), bf16[128,512]{1,0:T(8,128)(2,1)}) %all-reduce.2.cloned.1.call-update) | async-done | bytes 131088 | tf_op jit(solution)/shard_map/psum | solution.py:182
  58.3 4.3 %convert_multiply_fusion.3 = (f32[128,4096]{1,0:T(8,128)S(1)}, f32[4096]{0:T(1024)S(1)}, f32[128,4096]{1,0:T(8,128)S(1)}) fusion(bf16[128,4096]{1,0:T(8,128)(2,1)S(1)} %multiply_convert_fusion, f32[4096]{0:T(1024)S(1)} %copy-done.27, bf16[512,4096]{1,0:T(8,128)(2,1)} %param.34, bf16[128,512]{1,0:T(8,128)(2,1)} %all-reduce.2.cloned.1.call-done, ...), kind=kOutput, calls=%fused_computation.369 | convolution fusion | flops 542371840 | bytes 9603584 | tf_op jit(solution)/shard_map/dot_general | solution.py:187
  62.5 11.3 %broadcast_multiply_fusion = f32[4,32,16,4096]{3,2,1,0:T(8,128)} fusion(f32[4,32,16]{2,1,0:T(8,128)S(1)} %bitcast.1184, f32[4,32,4096]{2,1,0:T(8,128)S(1)} %bitcast.1144), kind=kLoop, calls=%fused_computation.356 | loop fusion | flops 8388608 | bytes 35659776 | tf_op jit(solution)/shard_map/mul | solution.py:126
  73.8 11.3 %multiply_exponential_fusion = f32[4,32,16,4096]{3,2,1,0:T(8,128)} fusion(f32[16,4096]{1,0:T(8,128)S(1)} %negate_bitcast_fusion, f32[4,32,4096]{2,1,0:T(8,128)S(1)} %bitcast.1143), kind=kLoop, calls=%fused_computation.355 | loop fusion | flops 8388608 | bytes 35913728 | tf_op jit(solution)/shard_map/exp | solution.py:125
  85.1 26.6 %while.37 = (s32[]{:T(128)}, f32[16,4096]{1,0:T(8,128)S(1)}, f32[4,32,16,4096]{3,2,1,0:T(8,128)}, f32[4,32,16,4096]{3,2,1,0:T(8,128)}, s32[]{:T(128)}, /*index=5...) while((s32[]{:T(128)}, f32[16,4096]{1,0:T(8,128)S(1)}, ...), condition=%wide.region_10.11_spmd.clone, body=%wide.region_9.10_spmd.clone.sunk | while | flops 4259874 | bytes 17302328 | solution.py:141
  85.1 6.6 %fusion.246 = f32[16,4096]{1,0:T(8,128)S(1)} fusion(f32[4,32,16,4096]{3,2,1,0:T(8,128)} %get-tuple-element.640, s32[]{:T(128)} %get-tuple-element.600, s32[]{:T(128)S(6)} %add.959, s32[]{:T(128)S(6)} %add.960, s32[]{:T(128)S(6)} %add.961, s32[]{:T(128)S(6)} %add.962, s32[]{:T(128)S(6)} %add.963, s32[]{:T(128)S(6)} %add.964, s32[]{:T(128)S(6)} %add.965, ...), kind=kLoop, calls=%fused_computation.228.clone.1 | loop fusion | flops 4259840 | bytes 17301632 | tf_op jit(solution)/shard_map/while/body/eval_jaxpr/add | solution.py:132
  91.8 6.6 %fusion.246 = f32[16,4096]{1,0:T(8,128)S(1)} fusion(f32[4,32,16,4096]{3,2,1,0:T(8,128)} %get-tuple-element.640, s32[]{:T(128)} %get-tuple-element.600, s32[]{:T(128)S(6)} %add.959, s32[]{:T(128)S(6)} %add.960, s32[]{:T(128)S(6)} %add.961, s32[]{:T(128)S(6)} %add.962, s32[]{:T(128)S(6)} %add.963, s32[]{:T(128)S(6)} %add.964, s32[]{:T(128)S(6)} %add.965, ...), kind=kLoop, calls=%fused_computation.228.clone.1 | loop fusion | flops 4259840 | bytes 17301632 | tf_op jit(solution)/shard_map/while/body/eval_jaxpr/add | solution.py:132
  98.4 6.6 %fusion.246 = f32[16,4096]{1,0:T(8,128)S(1)} fusion(f32[4,32,16,4096]{3,2,1,0:T(8,128)} %get-tuple-element.640, s32[]{:T(128)} %get-tuple-element.600, s32[]{:T(128)S(6)} %add.959, s32[]{:T(128)S(6)} %add.960, s32[]{:T(128)S(6)} %add.961, s32[]{:T(128)S(6)} %add.962, s32[]{:T(128)S(6)} %add.963, s32[]{:T(128)S(6)} %add.964, s32[]{:T(128)S(6)} %add.965, ...), kind=kLoop, calls=%fused_computation.228.clone.1 | loop fusion | flops 4259840 | bytes 17301632 | tf_op jit(solution)/shard_map/while/body/eval_jaxpr/add | solution.py:132
  105.1 6.6 %fusion.246 = f32[16,4096]{1,0:T(8,128)S(1)} fusion(f32[4,32,16,4096]{3,2,1,0:T(8,128)} %get-tuple-element.640, s32[]{:T(128)} %get-tuple-element.600, s32[]{:T(128)S(6)} %add.959, s32[]{:T(128)S(6)} %add.960, s32[]{:T(128)S(6)} %add.961, s32[]{:T(128)S(6)} %add.962, s32[]{:T(128)S(6)} %add.963, s32[]{:T(128)S(6)} %add.964, s32[]{:T(128)S(6)} %add.965, ...), kind=kLoop, calls=%fused_computation.228.clone.1 | loop fusion | flops 4259840 | bytes 17301632 | tf_op jit(solution)/shard_map/while/body/eval_jaxpr/add | solution.py:132
  112.5 1.3 fusion.195
  114.9 26.7 %all_gather.18 = bf16[1024,256]{0,1:T(8,128)(2,1)S(1)} all-gather(bf16[128,256]{0,1:T(8,128)(2,1)S(1)} %copy.47), channel_id=1, replica_groups=mesh['ctx'=8,'head'=4] {'ctx'}, dimensions={0}, use_global_device_ids=true | all-gather | bytes 589824 | tf_op jit(solution)/shard_map/all_gather | solution.py:109
  141.6 4.7 %fusion.160 = (f32[2,8,128]{2,1,0:T(8,128)S(1)}, f32[2,1024,128,8]{2,1,3,0:T(8,128)}) fusion(pred[128,1024]{0,1:T(8,128)(4,1)S(1)} %compare_and_fusion, bf16[1024,2,128,1]{0,2,3,1:T(8,128)(2,1)S(1)} %bitcast.1146, bf16[128,2,8,128]{3,2,1,0:T(8,128)(2,1)S(1)} %bitcast.1145), kind=kOutput, calls=%fused_computation.359 | convolution fusion | flops 543160320 | bytes 9576448 | tf_op jit(solution)/shard_map/rkgd,mkd->kgrm/dot_general | solution.py:61
  147.0 31.7 %all_gather.19 = bf16[1024,256]{1,0:T(8,128)(2,1)S(1)} all-gather(bf16[128,256]{1,0:T(8,128)(2,1)S(1)} %constant_dynamic-slice_fusion.32), channel_id=1, replica_groups=mesh['ctx'=8,'head'=4] {'ctx'}, dimensions={0}, use_global_device_ids=true | all-gather | bytes 589824 | tf_op jit(solution)/shard_map/all_gather | solution.py:110
  178.9 4.7 %fusion.161 = f32[2,8,128]{2,1,0:T(8,128)S(1)} fusion(f32[2,1024,128,8]{2,1,3,0:T(8,128)} %get-tuple-element.279, f32[2,8,128]{2,1,0:T(8,128)S(1)} %broadcast_maximum_fusion, pred[128,1024]{0,1:T(8,128)(4,1)S(1)} %compare_and_fusion), kind=kLoop, calls=%fused_computation.361 | loop fusion | flops 10483712 | bytes 8536064 | tf_op jit(solution)/shard_map/reduce_sum | solution.py:68
  183.7 1.2 copy-done.2
  184.9 2.2 divide_convert_fusion
  188.8 5.2 %all-gather.5.cloned.1.call-done = bf16[128,4096]{1,0:T(8,128)(2,1)} async-done(((bf16[16,4096]{1,0:T(8,128)(2,1)}), bf16[128,4096]{1,0:T(8,128)(2,1)}) %all-gather.5.cloned.1.call-update) | async-done | bytes 1048592 | tf_op jit(solution)/shard_map/all_gather | solution.py:16
  194.0 7.6 %while.35 = (s32[]{:T(128)}, f32[16,4096]{1,0:T(8,128)S(1)}, s32[]{:T(128)}, bf16[8,16,4096]{2,1,0:T(8,128)(2,1)}, bf16[8,16,4096]{2,1,0:T(8,128)(2,1)}, /*index=5*/s32[]{:T(128)}, s32[]{:T(128)}, s32[]{:T(128)}) while((s32[]{:T(128)}, f32[16,4096]{1,0:T(8,128)S(1)}, s32[]{:T(128)}, bf16[8,16,4096]{2,1,0:T(8,128)(2,1)}, ...), condition=%wide.region_12.13_spmd, body=%wide.region_11.12_spmd.sunk | while | flops 262149 | bytes 786555 | solution.py:30
  201.6 81.9 %while.36 = (s32[]{:T(128)}, f32[16,4096]{1,0:T(8,128)S(1)}, f32[4,32,4096]{2,1,0:T(8,128)}, f32[4,32,16,4096]{3,2,1,0:T(8,128)}, f32[4,32,16,4096]{3,2,1,0:T(8,...) while((s32[]{:T(128)}, f32[16,4096]{1,0:T(8,128)S(1)}, ...), condition=%wide.region_46.47_spmd, body=%wide.region_13.46_spmd.sunk | while | flops 8388641 | bytes 36451320 | solution.py:141
  201.6 1.7 fusion.245
  204.5 1.6 fusion.244
  206.1 7.9 %multiply_reduce_fusion.49 = (f32[4096]{0:T(1024)S(1)}, f32[16,4096]{1,0:T(8,128)S(1)}, f32[16,4096]{1,0:T(8,128)}, f32[16,4096]{1,0:T(8,128)}, f32[16,4096]{1,0...) fusion(f32[16]{0:T(128)S(1)} %get-tuple-element.465, ...), kind=kLoop, calls=%fused_computation.131.clone.1 | loop fusion | flops 4321280 | bytes 25182400 | tf_op jit(solution)/shard_map/while/body/eval_jaxpr/reduce_sum | solution.py:133
  214.0 1.2 multiply_reduce_fusion.65
  215.3 1.2 multiply_reduce_fusion.64
  216.5 1.2 multiply_reduce_fusion.63
  222.1 1.6 fusion.245
  224.9 1.6 fusion.244
  226.5 7.9 %multiply_reduce_fusion.49 = (f32[4096]{0:T(1024)S(1)}, f32[16,4096]{1,0:T(8,128)S(1)}, f32[16,4096]{1,0:T(8,128)}, f32[16,4096]{1,0:T(8,128)}, f32[16,4096]{1,0...) fusion(f32[16]{0:T(128)S(1)} %get-tuple-element.465, ...), kind=kLoop, calls=%fused_computation.131.clone.1 | loop fusion | flops 4321280 | bytes 25182400 | tf_op jit(solution)/shard_map/while/body/eval_jaxpr/reduce_sum | solution.py:133
  234.5 1.2 multiply_reduce_fusion.65
  235.7 1.2 multiply_reduce_fusion.64
  236.9 1.2 multiply_reduce_fusion.63
  242.6 1.6 fusion.245
  245.4 1.6 fusion.244
  247.0 7.9 %multiply_reduce_fusion.49 = (f32[4096]{0:T(1024)S(1)}, f32[16,4096]{1,0:T(8,128)S(1)}, f32[16,4096]{1,0:T(8,128)}, f32[16,4096]{1,0:T(8,128)}, f32[16,4096]{1,0...) fusion(f32[16]{0:T(128)S(1)} %get-tuple-element.465, ...), kind=kLoop, calls=%fused_computation.131.clone.1 | loop fusion | flops 4321280 | bytes 25182400 | tf_op jit(solution)/shard_map/while/body/eval_jaxpr/reduce_sum | solution.py:133
  255.0 1.2 multiply_reduce_fusion.65
  256.2 1.2 multiply_reduce_fusion.64
  257.4 1.2 multiply_reduce_fusion.63
  263.0 1.6 fusion.245
  265.8 1.6 fusion.244
  267.4 7.9 %multiply_reduce_fusion.49 = (f32[4096]{0:T(1024)S(1)}, f32[16,4096]{1,0:T(8,128)S(1)}, f32[16,4096]{1,0:T(8,128)}, f32[16,4096]{1,0:T(8,128)}, f32[16,4096]{1,0...) fusion(f32[16]{0:T(128)S(1)} %get-tuple-element.465, ...), kind=kLoop, calls=%fused_computation.131.clone.1 | loop fusion | flops 4321280 | bytes 25182400 | tf_op jit(solution)/shard_map/while/body/eval_jaxpr/reduce_sum | solution.py:133
  275.4 1.2 multiply_reduce_fusion.65
  276.6 1.2 multiply_reduce_fusion.64
  277.8 1.2 multiply_reduce_fusion.63
  283.5 4.0 %fusion.168 = bf16[128,4096]{1,0:T(8,128)(2,1)} fusion(bf16[128,4096]{1,0:T(8,128)(2,1)} %copy-done.3, bf16[128,4096]{1,0:T(8,128)(2,1)} %param.28, f32[4,32,4096]{2,1,0:T(8,128)} %get-tuple-element.102, f32[4096]{0:T(1024)} %param.37), kind=kLoop, calls=%fused_computation.372 | loop fusion | flops 5242880 | bytes 5259264 | tf_op jit(solution)/shard_map/convert_element_type | solution.py:200
  (286 shorter events, 42.1 us)
Async XLA Ops:
  7.2 7.5 %copy-start = (bf16[128,1024]{1,0:T(8,128)(2,1)S(1)}, bf16[128,1024]{1,0:T(8,128)(2,1)}, u32[]{:S(2)}) copy-start(bf16[128,1024]{1,0:T(8,128)(2,1)} %param.23) | copy-start | bytes 786436
  7.2 50.0 %all-reduce.2.cloned.1.call-start = ((), (), s32[]{:S(2)}) async-start(), calls=%async_computation | async-start | bytes 262144 | tf_op jit(solution)/shard_map/psum | solution.py:182
  8.1 7.5 %collective-permute-start = (bf16[3,4096]{1,0:T(4,128)(2,1)S(1)}, bf16[3,4096]{1,0:T(4,128)(2,1)S(1)}, u32[]{:S(2)}, u32[]{:S(2)}) collective-permute-start(bf16[3,4096]{1,0:T(4,128)(2,1)S(1)} %slice.693), channel_id=1, source_target_pairs={{0,4},{4,8},{8,12},{12,16},{16,20},{20,24},{24,28},{1,5},{5,9},{9,... | collective-permute-start | bytes 73736 | tf_op jit(solution)/shard_map/ppermute | solution.py:36
  19.1 39.1 %copy-start.3 = (bf16[128,4096]{1,0:T(8,128)(2,1)}, bf16[128,4096]{1,0:T(8,128)(2,1)S(1)}, u32[]{:S(2)}) copy-start(bf16[128,4096]{1,0:T(8,128)(2,1)S(1)} %multiply_convert_fusion) | copy-start | bytes 3145732
  19.1 4.1 %copy-start.6 = (bf16[4096,32]{0,1:T(8,128)(2,1)S(1)}, bf16[4096,32]{0,1:T(8,128)(2,1)}, u32[]{:S(2)}) copy-start(bf16[4096,32]{0,1:T(8,128)(2,1)} %param.32) | copy-start | bytes 786436
  19.1 39.1 %copy-start.27 = (f32[4096]{0:T(1024)S(1)}, f32[4096]{0:T(1024)}, u32[]{:S(2)}) copy-start(f32[4096]{0:T(1024)} %param.35) | copy-start | bytes 49156
  19.1 39.1 %copy-start.28 = (f32[512]{0:T(512)S(1)}, f32[512]{0:T(512)}, u32[]{:S(2)}) copy-start(f32[512]{0:T(512)} %param.33) | copy-start | bytes 6148
  23.1 165.6 %all-gather.7.cloned.1.call-start = ((), (), s32[]{:S(2)}) async-start(), calls=%async_computation.2 | async-start | bytes 1179648 | tf_op jit(solution)/shard_map/all_gather | solution.py:16
  85.1 28.7 %copy-start.5 = (bf16[128,2048]{1,0:T(8,128)(2,1)S(1)}, bf16[128,2048]{1,0:T(8,128)(2,1)}, u32[]{:S(2)}) copy-start(bf16[128,2048]{1,0:T(8,128)(2,1)} %param.22) | copy-start | bytes 1572868
  112.4 81.5 %all-gather.5.cloned.1.call-start = ((), (), s32[]{:S(2)}) async-start(), calls=%async_computation.1 | async-start | bytes 1179648 | tf_op jit(solution)/shard_map/all_gather | solution.py:16
  141.6 4.7 %copy-start.4 = (f32[4096,16]{0,1:T(8,128)S(1)}, f32[4096,16]{0,1:T(8,128)}, u32[]{:S(2)}) copy-start(f32[4096,16]{0,1:T(8,128)} %param.36) | copy-start | bytes 786436
  178.9 6.0 %copy-start.2 = (f32[2,1024,128,8]{2,1,3,0:T(8,128)S(1)}, f32[2,1024,128,8]{2,1,3,0:T(8,128)}, u32[]{:S(2)}) copy-start(f32[2,1024,128,8]{2,1,3,0:T(8,128)} %get-tuple-element.279) | copy-start | bytes 25165828
  214.0 4.5 %copy-start.12 = (f32[16]{0:T(128)S(1)}, f32[16]{0:T(128)}, u32[]{:S(2)}) copy-start(f32[16]{0:T(128)} %get-tuple-element.529) | copy-start | bytes 196 | tf_op jit(solution)/shard_map/while
  214.0 4.5 %copy-start.13 = (f32[16]{0:T(128)S(1)}, f32[16]{0:T(128)}, u32[]{:S(2)}) copy-start(f32[16]{0:T(128)} %get-tuple-element.531) | copy-start | bytes 196 | tf_op jit(solution)/shard_map/while
  214.0 4.7 %copy-start.10 = (f32[16]{0:T(128)S(1)}, f32[16]{0:T(128)}, u32[]{:S(2)}) copy-start(f32[16]{0:T(128)} %get-tuple-element.523) | copy-start | bytes 196 | tf_op jit(solution)/shard_map/while
  214.0 4.7 %copy-start.11 = (f32[16]{0:T(128)S(1)}, f32[16]{0:T(128)}, u32[]{:S(2)}) copy-start(f32[16]{0:T(128)} %get-tuple-element.525) | copy-start | bytes 196 | tf_op jit(solution)/shard_map/while
  214.0 4.9 %copy-start.8 = (f32[16]{0:T(128)S(1)}, f32[16]{0:T(128)}, u32[]{:S(2)}) copy-start(f32[16]{0:T(128)} %get-tuple-element.517) | copy-start | bytes 196 | tf_op jit(solution)/shard_map/while
  214.0 4.9 %copy-start.9 = (f32[16]{0:T(128)S(1)}, f32[16]{0:T(128)}, u32[]{:S(2)}) copy-start(f32[16]{0:T(128)} %get-tuple-element.519) | copy-start | bytes 196 | tf_op jit(solution)/shard_map/while
  214.0 5.0 %copy-start.7 = (f32[16]{0:T(128)S(1)}, f32[16]{0:T(128)}, u32[]{:S(2)}) copy-start(f32[16]{0:T(128)} %get-tuple-element.513) | copy-start | bytes 196 | tf_op jit(solution)/shard_map/while
  215.2 4.0 %copy-start.25 = (f32[16]{0:T(128)S(1)}, f32[16]{0:T(128)}, u32[]{:S(2)}) copy-start(f32[16]{0:T(128)} %get-tuple-element.504) | copy-start | bytes 196 | tf_op jit(solution)/shard_map/while
  215.2 4.0 %copy-start.26 = (f32[16]{0:T(128)S(1)}, f32[16]{0:T(128)}, u32[]{:S(2)}) copy-start(f32[16]{0:T(128)} %get-tuple-element.506) | copy-start | bytes 196 | tf_op jit(solution)/shard_map/while
  234.4 4.5 %copy-start.12 = (f32[16]{0:T(128)S(1)}, f32[16]{0:T(128)}, u32[]{:S(2)}) copy-start(f32[16]{0:T(128)} %get-tuple-element.529) | copy-start | bytes 196 | tf_op jit(solution)/shard_map/while
  234.4 4.5 %copy-start.13 = (f32[16]{0:T(128)S(1)}, f32[16]{0:T(128)}, u32[]{:S(2)}) copy-start(f32[16]{0:T(128)} %get-tuple-element.531) | copy-start | bytes 196 | tf_op jit(solution)/shard_map/while
  234.4 4.7 %copy-start.10 = (f32[16]{0:T(128)S(1)}, f32[16]{0:T(128)}, u32[]{:S(2)}) copy-start(f32[16]{0:T(128)} %get-tuple-element.523) | copy-start | bytes 196 | tf_op jit(solution)/shard_map/while
  234.5 4.7 %copy-start.11 = (f32[16]{0:T(128)S(1)}, f32[16]{0:T(128)}, u32[]{:S(2)}) copy-start(f32[16]{0:T(128)} %get-tuple-element.525) | copy-start | bytes 196 | tf_op jit(solution)/shard_map/while
  234.5 4.9 %copy-start.8 = (f32[16]{0:T(128)S(1)}, f32[16]{0:T(128)}, u32[]{:S(2)}) copy-start(f32[16]{0:T(128)} %get-tuple-element.517) | copy-start | bytes 196 | tf_op jit(solution)/shard_map/while
  234.5 4.9 %copy-start.9 = (f32[16]{0:T(128)S(1)}, f32[16]{0:T(128)}, u32[]{:S(2)}) copy-start(f32[16]{0:T(128)} %get-tuple-element.519) | copy-start | bytes 196 | tf_op jit(solution)/shard_map/while
  234.5 5.0 %copy-start.7 = (f32[16]{0:T(128)S(1)}, f32[16]{0:T(128)}, u32[]{:S(2)}) copy-start(f32[16]{0:T(128)} %get-tuple-element.513) | copy-start | bytes 196 | tf_op jit(solution)/shard_map/while
  235.7 4.0 %copy-start.25 = (f32[16]{0:T(128)S(1)}, f32[16]{0:T(128)}, u32[]{:S(2)}) copy-start(f32[16]{0:T(128)} %get-tuple-element.504) | copy-start | bytes 196 | tf_op jit(solution)/shard_map/while
  235.7 4.0 %copy-start.26 = (f32[16]{0:T(128)S(1)}, f32[16]{0:T(128)}, u32[]{:S(2)}) copy-start(f32[16]{0:T(128)} %get-tuple-element.506) | copy-start | bytes 196 | tf_op jit(solution)/shard_map/while
  254.9 4.5 %copy-start.12 = (f32[16]{0:T(128)S(1)}, f32[16]{0:T(128)}, u32[]{:S(2)}) copy-start(f32[16]{0:T(128)} %get-tuple-element.529) | copy-start | bytes 196 | tf_op jit(solution)/shard_map/while
  254.9 4.5 %copy-start.13 = (f32[16]{0:T(128)S(1)}, f32[16]{0:T(128)}, u32[]{:S(2)}) copy-start(f32[16]{0:T(128)} %get-tuple-element.531) | copy-start | bytes 196 | tf_op jit(solution)/shard_map/while
  254.9 4.7 %copy-start.10 = (f32[16]{0:T(128)S(1)}, f32[16]{0:T(128)}, u32[]{:S(2)}) copy-start(f32[16]{0:T(128)} %get-tuple-element.523) | copy-start | bytes 196 | tf_op jit(solution)/shard_map/while
  254.9 4.7 %copy-start.11 = (f32[16]{0:T(128)S(1)}, f32[16]{0:T(128)}, u32[]{:S(2)}) copy-start(f32[16]{0:T(128)} %get-tuple-element.525) | copy-start | bytes 196 | tf_op jit(solution)/shard_map/while
  255.0 4.9 %copy-start.8 = (f32[16]{0:T(128)S(1)}, f32[16]{0:T(128)}, u32[]{:S(2)}) copy-start(f32[16]{0:T(128)} %get-tuple-element.517) | copy-start | bytes 196 | tf_op jit(solution)/shard_map/while
  255.0 4.9 %copy-start.9 = (f32[16]{0:T(128)S(1)}, f32[16]{0:T(128)}, u32[]{:S(2)}) copy-start(f32[16]{0:T(128)} %get-tuple-element.519) | copy-start | bytes 196 | tf_op jit(solution)/shard_map/while
  255.0 5.0 %copy-start.7 = (f32[16]{0:T(128)S(1)}, f32[16]{0:T(128)}, u32[]{:S(2)}) copy-start(f32[16]{0:T(128)} %get-tuple-element.513) | copy-start | bytes 196 | tf_op jit(solution)/shard_map/while
  256.2 4.0 %copy-start.25 = (f32[16]{0:T(128)S(1)}, f32[16]{0:T(128)}, u32[]{:S(2)}) copy-start(f32[16]{0:T(128)} %get-tuple-element.504) | copy-start | bytes 196 | tf_op jit(solution)/shard_map/while
  256.2 4.0 %copy-start.26 = (f32[16]{0:T(128)S(1)}, f32[16]{0:T(128)}, u32[]{:S(2)}) copy-start(f32[16]{0:T(128)} %get-tuple-element.506) | copy-start | bytes 196 | tf_op jit(solution)/shard_map/while
  275.3 4.5 %copy-start.12 = (f32[16]{0:T(128)S(1)}, f32[16]{0:T(128)}, u32[]{:S(2)}) copy-start(f32[16]{0:T(128)} %get-tuple-element.529) | copy-start | bytes 196 | tf_op jit(solution)/shard_map/while
  275.3 4.5 %copy-start.13 = (f32[16]{0:T(128)S(1)}, f32[16]{0:T(128)}, u32[]{:S(2)}) copy-start(f32[16]{0:T(128)} %get-tuple-element.531) | copy-start | bytes 196 | tf_op jit(solution)/shard_map/while
  275.4 4.7 %copy-start.10 = (f32[16]{0:T(128)S(1)}, f32[16]{0:T(128)}, u32[]{:S(2)}) copy-start(f32[16]{0:T(128)} %get-tuple-element.523) | copy-start | bytes 196 | tf_op jit(solution)/shard_map/while
  275.4 4.7 %copy-start.11 = (f32[16]{0:T(128)S(1)}, f32[16]{0:T(128)}, u32[]{:S(2)}) copy-start(f32[16]{0:T(128)} %get-tuple-element.525) | copy-start | bytes 196 | tf_op jit(solution)/shard_map/while
  275.4 4.9 %copy-start.8 = (f32[16]{0:T(128)S(1)}, f32[16]{0:T(128)}, u32[]{:S(2)}) copy-start(f32[16]{0:T(128)} %get-tuple-element.517) | copy-start | bytes 196 | tf_op jit(solution)/shard_map/while
  275.4 4.9 %copy-start.9 = (f32[16]{0:T(128)S(1)}, f32[16]{0:T(128)}, u32[]{:S(2)}) copy-start(f32[16]{0:T(128)} %get-tuple-element.519) | copy-start | bytes 196 | tf_op jit(solution)/shard_map/while
  275.4 5.0 %copy-start.7 = (f32[16]{0:T(128)S(1)}, f32[16]{0:T(128)}, u32[]{:S(2)}) copy-start(f32[16]{0:T(128)} %get-tuple-element.513) | copy-start | bytes 196 | tf_op jit(solution)/shard_map/while
  276.6 4.0 %copy-start.25 = (f32[16]{0:T(128)S(1)}, f32[16]{0:T(128)}, u32[]{:S(2)}) copy-start(f32[16]{0:T(128)} %get-tuple-element.504) | copy-start | bytes 196 | tf_op jit(solution)/shard_map/while
  276.6 4.0 %copy-start.26 = (f32[16]{0:T(128)S(1)}, f32[16]{0:T(128)}, u32[]{:S(2)}) copy-start(f32[16]{0:T(128)} %get-tuple-element.506) | copy-start | bytes 196 | tf_op jit(solution)/shard_map/while
  (45 other events, 79.7 us)
Sparse Core Ops, SparseCore 0:
  23.3 33.9 all-reduce.1
  112.6 39.1 all-gather.6
  153.9 39.9 all-gather.4
where the time goes:
time: 295 us; the launch traced here: 294 us
  other arithmetic  137 us (46%)
  blocking collectives  65.5 us (22%)
  waiting for transfers between devices  31.6 us (11%)
  local copies, waits for them, and re-layouts  27.7 us (9%)
  matrix products  15.5 us (5%)
  between operations  14.1 us (5%)
    reduce_sum x68, other arithmetic, one_block(): results.append(jnp.sum(state * c_block[offset][:, None], axis=0))  60.4 us
    all_gather x1, blocking collectives, attention(): lax.all_gather(value_mine, 'ctx', axis=0, tiled=True)  31.7 us
    all_gather x1, blocking collectives, attention(): lax.all_gather(key_mine, 'ctx', axis=0, tiled=True)  26.7 us
    add x4, other arithmetic, one_block(): state = decay_block[offset] * state + drive_block[offset]  26.5 us
    psum x1, waiting for transfers between devices, mamba(): lax.psum(low_part.astype(jnp.bfloat16), 'head').astype(jnp.float32)  26.4 us
    mul x8, local copies, waits for them, and re-layouts, one_block(): results.append(jnp.sum(state * c_block[offset][:, None], axis=0))  13.1 us
    exp x1, other arithmetic, local_scan(): decay_all = jnp.exp(step_dt[:, None, :] * rate_table[None])  11.3 us
    mul x1, other arithmetic, local_scan(): drive_all = (step_dt * inputs_f)[:, None, :] * b_vals[:, :, None]  11.3 us
  transfers between devices with their start and end apart: 4, of which 2 were waited for; matrix products, arithmetic and copies ran while one was open for 8% of the time, Pallas kernels for 0%

commit v1 on v0

--- a/solution.py
+++ b/solution.py
@@ -8,6 +8,11 @@
 STATE = 16
 CONV = 4
 NEG_FILL = -1e30
+
+
+def add_all(x, axis):
+    parts = lax.all_gather(x, axis)
+    return jnp.sum(parts, axis=0)
 
 
 def prefix(shard, axis, join, neutral):
@@ -179,7 +184,7 @@
     low_part = jnp.dot(act_bf, low_weight, preferred_element_type=jnp.float32)
     bc_part = jnp.dot(act_bf, bc_weight, preferred_element_type=jnp.float32)
     low_sum, bc_sum = (
-        lax.psum(low_part.astype(jnp.bfloat16), "head").astype(jnp.float32),
+        add_all(low_part.astype(jnp.bfloat16), "head").astype(jnp.float32),
         lax.psum(bc_part.astype(jnp.bfloat16), "head").astype(jnp.float32),
     )
     normed = normalize(low_sum, low_gain)

time: 295 us -> 277 us (0.939)
  waiting for transfers between devices: 31.6 us -> 6.76 us
  blocking collectives: 65.5 us -> 73.3 us
    psum x1 -> x0, waiting for transfers between devices: 26.4 us -> none  [mamba(): lax.psum(low_part.astype(jnp.bfloat16), 'head').astype(jnp.float32)]
    all_gather x0 -> x1, blocking collectives: none -> 7.2 us  [add_all(): parts = lax.all_gather(x, axis)]
  transfers between devices with their start and end apart: 4 -> 3, of which waited for: 2 -> 1; matrix products, arithmetic and copies ran while one was open for 8% -> 8% of each run, Pallas kernels for 0% -> 0%
where the time goes in v1:
time: 277 us; the launch traced here: 276 us
  other arithmetic  136 us (49%)
  blocking collectives  73.3 us (26%)
  local copies, waits for them, and re-layouts  27.9 us (10%)
  matrix products  14.7 us (5%)
  between operations  14.4 us (5%)
  waiting for transfers between devices  6.76 us (2%)
    reduce_sum x68, other arithmetic, one_block(): results.append(jnp.sum(state * c_block[offset][:, None], axis=0))  60.4 us
    all_gather x1, blocking collectives, attention(): lax.all_gather(value_mine, 'ctx', axis=0, tiled=True)  31.7 us
    all_gather x1, blocking collectives, attention(): lax.all_gather(key_mine, 'ctx', axis=0, tiled=True)  27.6 us
    add x4, other arithmetic, one_block(): state = decay_block[offset] * state + drive_block[offset]  26.5 us
    mul x8, local copies, waits for them, and re-layouts, one_block(): results.append(jnp.sum(state * c_block[offset][:, None], axis=0))  13.1 us
    exp x1, other arithmetic, local_scan(): decay_all = jnp.exp(step_dt[:, None, :] * rate_table[None])  11.3 us
    mul x1, other arithmetic, local_scan(): drive_all = (step_dt * inputs_f)[:, None, :] * b_vals[:, :, None]  11.3 us
    add x7, other arithmetic, link(): return (earlier[0] * later[0], earlier[1] * later[0] + later[1])  7.45 us
  transfers between devices with their start and end apart: 3, of which 1 were waited for; matrix products, arithmetic and copies ran while one was open for 8% of the time, Pallas kernels for 0%

profile of v1, /device:TPU:26, one launch (start us, length us, event | category | flops | bytes accessed | tf_op | source)
XLA Modules:
  0.0 275.8 jit_solution(17478535288300803043)
XLA Ops:
  8.1 1.3 collective-permute-start
  15.7 3.5 %multiply_convert_fusion = bf16[128,4096]{1,0:T(8,128)(2,1)S(1)} fusion(bf16[128,4096]{1,0:T(8,128)(2,1)} %param.27, bf16[3,4096]{1,0:T(4,128)(2,1)S(1)} %collective-permute-done, f32[4096]{0:T(1024)S(1)} %bitcast.1189, f32[4096]{0:T(1024)S(1)} %bitcast.1190, f32[4096]{0:T(1024)S(1)} %bitcast.1188, f32[4096]{0:T(1024)S(1)} %bitcast.1187, f32[4096]{0:T(1024)} %param.30), kind=kLoop, calls=%fused_computation.376 | loop fusion | flops 13631488 | bytes 2203648 | tf_op jit(solution)/shard_map/convert_element_type | solution.py:183
  19.2 3.3 %convolution_convert_fusion = bf16[128,512]{1,0:T(8,128)(2,1)S(1)} fusion(bf16[128,4096]{1,0:T(8,128)(2,1)S(1)} %multiply_convert_fusion, bf16[4096,512]{1,0:T(8,128)(2,1)} %param.31), kind=kOutput, calls=%fused_computation.380 | convolution fusion | flops 536936448 | bytes 5373952 | tf_op jit(solution)/shard_map/dot_general | solution.py:184
  22.5 7.2 %all-gather = bf16[512,512]{1,0:T(8,128)(2,1)S(1)} all-gather(bf16[128,512]{1,0:T(8,128)(2,1)S(1)} %convolution_convert_fusion), channel_id=2, replica_groups=mesh['ctx'=8,'head'=4] {'head'}, dimensions={0}, use_global_device_ids=true | all-gather | bytes 655360 | tf_op jit(solution)/shard_map/all_gather | solution.py:14
  30.4 6.8 %psum.7 = bf16[128,32]{0,1:T(8,128)(2,1)S(1)} all-reduce(bf16[128,32]{0,1:T(8,128)(2,1)S(1)} %convolution_convert_fusion.1), channel_id=1, replica_groups=mesh['ctx'=8,'head'=4] {'head'}, use_global_device_ids=true, to_apply=%region_8.9 | all-reduce | flops 4096 | bytes 16384 | tf_op jit(solution)/shard_map/psum | solution.py:188
  37.3 4.2 %convert_multiply_fusion.3 = (f32[128,4096]{1,0:T(8,128)S(1)}, f32[4096]{0:T(1024)S(1)}, f32[128,4096]{1,0:T(8,128)S(1)}) fusion(bf16[128,4096]{1,0:T(8,128)(2,1)S(1)} %multiply_convert_fusion, f32[4096]{0:T(1024)S(1)} %copy-done.27, bf16[512,4096]{1,0:T(8,128)(2,1)} %param.34, bf16[128,512]{1,0:T(8,128)(2,1)S(1)} %reduce_sum.358, f32[512]{0:T(512)S(1)} %copy-done.28, ...), kind=kOutput, calls=%fused_computation.369 | convolution fusion | flops 542371840 | bytes 9603584 | tf_op jit(solution)/shard_map/dot_general | solution.py:192
  41.5 11.3 %broadcast_multiply_fusion = f32[4,32,16,4096]{3,2,1,0:T(8,128)} fusion(f32[4,32,16]{2,1,0:T(8,128)S(1)} %bitcast.1186, f32[4,32,4096]{2,1,0:T(8,128)S(1)} %bitcast.1145), kind=kLoop, calls=%fused_computation.356 | loop fusion | flops 8388608 | bytes 35659776 | tf_op jit(solution)/shard_map/mul | solution.py:131
  52.8 11.3 %multiply_exponential_fusion = f32[4,32,16,4096]{3,2,1,0:T(8,128)} fusion(f32[16,4096]{1,0:T(8,128)S(1)} %negate_bitcast_fusion, f32[4,32,4096]{2,1,0:T(8,128)S(1)} %bitcast.1144), kind=kLoop, calls=%fused_computation.355 | loop fusion | flops 8388608 | bytes 35913728 | tf_op jit(solution)/shard_map/exp | solution.py:130
  64.1 26.6 %while.37 = (s32[]{:T(128)}, f32[16,4096]{1,0:T(8,128)S(1)}, f32[4,32,16,4096]{3,2,1,0:T(8,128)}, f32[4,32,16,4096]{3,2,1,0:T(8,128)}, s32[]{:T(128)}, /*index=5...) while((s32[]{:T(128)}, f32[16,4096]{1,0:T(8,128)S(1)}, ...), condition=%wide.region_10.11_spmd.clone, body=%wide.region_9.10_spmd.clone.sunk | while | flops 4259874 | bytes 17302328 | solution.py:146
  64.1 6.6 %fusion.246 = f32[16,4096]{1,0:T(8,128)S(1)} fusion(f32[4,32,16,4096]{3,2,1,0:T(8,128)} %get-tuple-element.640, s32[]{:T(128)} %get-tuple-element.600, s32[]{:T(128)S(6)} %add.957, s32[]{:T(128)S(6)} %add.958, s32[]{:T(128)S(6)} %add.959, s32[]{:T(128)S(6)} %add.960, s32[]{:T(128)S(6)} %add.961, s32[]{:T(128)S(6)} %add.962, s32[]{:T(128)S(6)} %add.963, ...), kind=kLoop, calls=%fused_computation.228.clone.1 | loop fusion | flops 4259840 | bytes 17301632 | tf_op jit(solution)/shard_map/while/body/eval_jaxpr/add | solution.py:137
  70.7 6.6 %fusion.246 = f32[16,4096]{1,0:T(8,128)S(1)} fusion(f32[4,32,16,4096]{3,2,1,0:T(8,128)} %get-tuple-element.640, s32[]{:T(128)} %get-tuple-element.600, s32[]{:T(128)S(6)} %add.957, s32[]{:T(128)S(6)} %add.958, s32[]{:T(128)S(6)} %add.959, s32[]{:T(128)S(6)} %add.960, s32[]{:T(128)S(6)} %add.961, s32[]{:T(128)S(6)} %add.962, s32[]{:T(128)S(6)} %add.963, ...), kind=kLoop, calls=%fused_computation.228.clone.1 | loop fusion | flops 4259840 | bytes 17301632 | tf_op jit(solution)/shard_map/while/body/eval_jaxpr/add | solution.py:137
  77.4 6.6 %fusion.246 = f32[16,4096]{1,0:T(8,128)S(1)} fusion(f32[4,32,16,4096]{3,2,1,0:T(8,128)} %get-tuple-element.640, s32[]{:T(128)} %get-tuple-element.600, s32[]{:T(128)S(6)} %add.957, s32[]{:T(128)S(6)} %add.958, s32[]{:T(128)S(6)} %add.959, s32[]{:T(128)S(6)} %add.960, s32[]{:T(128)S(6)} %add.961, s32[]{:T(128)S(6)} %add.962, s32[]{:T(128)S(6)} %add.963, ...), kind=kLoop, calls=%fused_computation.228.clone.1 | loop fusion | flops 4259840 | bytes 17301632 | tf_op jit(solution)/shard_map/while/body/eval_jaxpr/add | solution.py:137
  84.1 6.6 %fusion.246 = f32[16,4096]{1,0:T(8,128)S(1)} fusion(f32[4,32,16,4096]{3,2,1,0:T(8,128)} %get-tuple-element.640, s32[]{:T(128)} %get-tuple-element.600, s32[]{:T(128)S(6)} %add.957, s32[]{:T(128)S(6)} %add.958, s32[]{:T(128)S(6)} %add.959, s32[]{:T(128)S(6)} %add.960, s32[]{:T(128)S(6)} %add.961, s32[]{:T(128)S(6)} %add.962, s32[]{:T(128)S(6)} %add.963, ...), kind=kLoop, calls=%fused_computation.228.clone.1 | loop fusion | flops 4259840 | bytes 17301632 | tf_op jit(solution)/shard_map/while/body/eval_jaxpr/add | solution.py:137
  91.5 1.3 fusion.195
  94.0 27.6 %all_gather.24 = bf16[1024,256]{0,1:T(8,128)(2,1)S(1)} all-gather(bf16[128,256]{0,1:T(8,128)(2,1)S(1)} %copy.47), channel_id=1, replica_groups=mesh['ctx'=8,'head'=4] {'ctx'}, dimensions={0}, use_global_device_ids=true | all-gather | bytes 589824 | tf_op jit(solution)/shard_map/all_gather | solution.py:114
  121.6 4.7 %fusion.160 = (f32[2,8,128]{2,1,0:T(8,128)S(1)}, f32[2,1024,128,8]{2,1,3,0:T(8,128)}) fusion(pred[128,1024]{0,1:T(8,128)(4,1)S(1)} %compare_and_fusion, bf16[1024,2,128,1]{0,2,3,1:T(8,128)(2,1)S(1)} %bitcast.1147, bf16[128,2,8,128]{3,2,1,0:T(8,128)(2,1)S(1)} %bitcast.1146), kind=kOutput, calls=%fused_computation.359 | convolution fusion | flops 543160320 | bytes 9576448 | tf_op jit(solution)/shard_map/rkgd,mkd->kgrm/dot_general | solution.py:66
  127.0 31.7 %all_gather.25 = bf16[1024,256]{1,0:T(8,128)(2,1)S(1)} all-gather(bf16[128,256]{1,0:T(8,128)(2,1)S(1)} %constant_dynamic-slice_fusion.32), channel_id=1, replica_groups=mesh['ctx'=8,'head'=4] {'ctx'}, dimensions={0}, use_global_device_ids=true | all-gather | bytes 589824 | tf_op jit(solution)/shard_map/all_gather | solution.py:115
  158.9 4.6 %fusion.161 = f32[2,8,128]{2,1,0:T(8,128)S(1)} fusion(f32[2,1024,128,8]{2,1,3,0:T(8,128)} %get-tuple-element.279, f32[2,8,128]{2,1,0:T(8,128)S(1)} %broadcast_maximum_fusion, pred[128,1024]{0,1:T(8,128)(4,1)S(1)} %compare_and_fusion), kind=kLoop, calls=%fused_computation.361 | loop fusion | flops 10483712 | bytes 8536064 | tf_op jit(solution)/shard_map/reduce_sum | solution.py:73
  163.5 1.4 copy-done.2
  164.8 2.2 divide_convert_fusion
  168.7 6.7 %all-gather.6.cloned.1.call-done = bf16[128,4096]{1,0:T(8,128)(2,1)} async-done(((bf16[16,4096]{1,0:T(8,128)(2,1)}), bf16[128,4096]{1,0:T(8,128)(2,1)}) %all-gather.6.cloned.1.call-update) | async-done | bytes 1048592 | tf_op jit(solution)/shard_map/all_gather | solution.py:21
  175.5 7.6 %while.35 = (s32[]{:T(128)}, f32[16,4096]{1,0:T(8,128)S(1)}, s32[]{:T(128)}, bf16[8,16,4096]{2,1,0:T(8,128)(2,1)}, bf16[8,16,4096]{2,1,0:T(8,128)(2,1)}, /*index=5*/s32[]{:T(128)}, s32[]{:T(128)}, s32[]{:T(128)}) while((s32[]{:T(128)}, f32[16,4096]{1,0:T(8,128)S(1)}, s32[]{:T(128)}, bf16[8,16,4096]{2,1,0:T(8,128)(2,1)}, ...), condition=%wide.region_12.13_spmd, body=%wide.region_11.12_spmd.sunk | while | flops 262149 | bytes 786555 | solution.py:35
  183.1 81.9 %while.36 = (s32[]{:T(128)}, f32[16,4096]{1,0:T(8,128)S(1)}, f32[4,32,4096]{2,1,0:T(8,128)}, f32[4,32,16,4096]{3,2,1,0:T(8,128)}, f32[4,32,16,4096]{3,2,1,0:T(8,...) while((s32[]{:T(128)}, f32[16,4096]{1,0:T(8,128)S(1)}, ...), condition=%wide.region_46.47_spmd, body=%wide.region_13.46_spmd.sunk | while | flops 8388641 | bytes 36451320 | solution.py:146
  183.1 1.7 fusion.245
  186.0 1.6 fusion.244
  187.6 7.9 %multiply_reduce_fusion.49 = (f32[4096]{0:T(1024)S(1)}, f32[16,4096]{1,0:T(8,128)S(1)}, f32[16,4096]{1,0:T(8,128)}, f32[16,4096]{1,0:T(8,128)}, f32[16,4096]{1,0...) fusion(f32[16]{0:T(128)S(1)} %get-tuple-element.465, ...), kind=kLoop, calls=%fused_computation.131.clone.1 | loop fusion | flops 4321280 | bytes 25182400 | tf_op jit(solution)/shard_map/while/body/eval_jaxpr/reduce_sum | solution.py:138
  195.6 1.2 multiply_reduce_fusion.65
  196.8 1.2 multiply_reduce_fusion.64
  198.0 1.2 multiply_reduce_fusion.63
  203.7 1.6 fusion.245
  206.4 1.6 fusion.244
  208.0 7.9 %multiply_reduce_fusion.49 = (f32[4096]{0:T(1024)S(1)}, f32[16,4096]{1,0:T(8,128)S(1)}, f32[16,4096]{1,0:T(8,128)}, f32[16,4096]{1,0:T(8,128)}, f32[16,4096]{1,0...) fusion(f32[16]{0:T(128)S(1)} %get-tuple-element.465, ...), kind=kLoop, calls=%fused_computation.131.clone.1 | loop fusion | flops 4321280 | bytes 25182400 | tf_op jit(solution)/shard_map/while/body/eval_jaxpr/reduce_sum | solution.py:138
  216.0 1.2 multiply_reduce_fusion.65
  217.2 1.2 multiply_reduce_fusion.64
  218.4 1.2 multiply_reduce_fusion.63
  224.1 1.6 fusion.245
  226.9 1.6 fusion.244
  228.5 7.9 %multiply_reduce_fusion.49 = (f32[4096]{0:T(1024)S(1)}, f32[16,4096]{1,0:T(8,128)S(1)}, f32[16,4096]{1,0:T(8,128)}, f32[16,4096]{1,0:T(8,128)}, f32[16,4096]{1,0...) fusion(f32[16]{0:T(128)S(1)} %get-tuple-element.465, ...), kind=kLoop, calls=%fused_computation.131.clone.1 | loop fusion | flops 4321280 | bytes 25182400 | tf_op jit(solution)/shard_map/while/body/eval_jaxpr/reduce_sum | solution.py:138
  236.5 1.2 multiply_reduce_fusion.65
  237.7 1.2 multiply_reduce_fusion.64
  238.9 1.2 multiply_reduce_fusion.63
  244.6 1.6 fusion.245
  247.3 1.6 fusion.244
  249.0 7.9 %multiply_reduce_fusion.49 = (f32[4096]{0:T(1024)S(1)}, f32[16,4096]{1,0:T(8,128)S(1)}, f32[16,4096]{1,0:T(8,128)}, f32[16,4096]{1,0:T(8,128)}, f32[16,4096]{1,0...) fusion(f32[16]{0:T(128)S(1)} %get-tuple-element.465, ...), kind=kLoop, calls=%fused_computation.131.clone.1 | loop fusion | flops 4321280 | bytes 25182400 | tf_op jit(solution)/shard_map/while/body/eval_jaxpr/reduce_sum | solution.py:138
  256.9 1.2 multiply_reduce_fusion.65
  258.1 1.2 multiply_reduce_fusion.64
  259.3 1.2 multiply_reduce_fusion.63
  265.0 4.0 %fusion.168 = bf16[128,4096]{1,0:T(8,128)(2,1)} fusion(bf16[128,4096]{1,0:T(8,128)(2,1)} %copy-done.3, bf16[128,4096]{1,0:T(8,128)(2,1)} %param.28, f32[4,32,4096]{2,1,0:T(8,128)} %get-tuple-element.102, f32[4096]{0:T(1024)} %param.37), kind=kLoop, calls=%fused_computation.372 | loop fusion | flops 5242880 | bytes 5259264 | tf_op jit(solution)/shard_map/convert_element_type | solution.py:205
  (285 shorter events, 41.3 us)
Async XLA Ops:
  7.2 7.6 %copy-start = (bf16[128,1024]{1,0:T(8,128)(2,1)S(1)}, bf16[128,1024]{1,0:T(8,128)(2,1)}, u32[]{:S(2)}) copy-start(bf16[128,1024]{1,0:T(8,128)(2,1)} %param.23) | copy-start | bytes 786436
  7.2 161.6 %all-gather.8.cloned.1.call-start = ((), (), s32[]{:S(2)}) async-start(), calls=%async_computation.1 | async-start | bytes 1179648 | tf_op jit(solution)/shard_map/all_gather | solution.py:21
  8.1 7.6 %collective-permute-start = (bf16[3,4096]{1,0:T(4,128)(2,1)S(1)}, bf16[3,4096]{1,0:T(4,128)(2,1)S(1)}, u32[]{:S(2)}, u32[]{:S(2)}) collective-permute-start(bf16[3,4096]{1,0:T(4,128)(2,1)S(1)} %slice.693), channel_id=1, source_target_pairs={{0,4},{4,8},{8,12},{12,16},{16,20},{20,24},{24,28},{1,5},{5,9},{9,... | collective-permute-start | bytes 73736 | tf_op jit(solution)/shard_map/ppermute | solution.py:41
  19.2 18.1 %copy-start.3 = (bf16[128,4096]{1,0:T(8,128)(2,1)}, bf16[128,4096]{1,0:T(8,128)(2,1)S(1)}, u32[]{:S(2)}) copy-start(bf16[128,4096]{1,0:T(8,128)(2,1)S(1)} %multiply_convert_fusion) | copy-start | bytes 3145732
  19.2 10.7 %copy-start.6 = (bf16[4096,32]{0,1:T(8,128)(2,1)S(1)}, bf16[4096,32]{0,1:T(8,128)(2,1)}, u32[]{:S(2)}) copy-start(bf16[4096,32]{0,1:T(8,128)(2,1)} %param.32) | copy-start | bytes 786436
  22.5 14.8 %copy-start.27 = (f32[4096]{0:T(1024)S(1)}, f32[4096]{0:T(1024)}, u32[]{:S(2)}) copy-start(f32[4096]{0:T(1024)} %param.35) | copy-start | bytes 49156
  22.5 14.8 %copy-start.28 = (f32[512]{0:T(512)S(1)}, f32[512]{0:T(512)}, u32[]{:S(2)}) copy-start(f32[512]{0:T(512)} %param.33) | copy-start | bytes 6148
  64.1 28.8 %copy-start.5 = (bf16[128,2048]{1,0:T(8,128)(2,1)S(1)}, bf16[128,2048]{1,0:T(8,128)(2,1)}, u32[]{:S(2)}) copy-start(bf16[128,2048]{1,0:T(8,128)(2,1)} %param.22) | copy-start | bytes 1572868
  91.4 84.0 %all-gather.6.cloned.1.call-start = ((), (), s32[]{:S(2)}) async-start(), calls=%async_computation | async-start | bytes 1179648 | tf_op jit(solution)/shard_map/all_gather | solution.py:21
  121.6 4.7 %copy-start.4 = (f32[4096,16]{0,1:T(8,128)S(1)}, f32[4096,16]{0,1:T(8,128)}, u32[]{:S(2)}) copy-start(f32[4096,16]{0,1:T(8,128)} %param.36) | copy-start | bytes 786436
  158.9 6.0 %copy-start.2 = (f32[2,1024,128,8]{2,1,3,0:T(8,128)S(1)}, f32[2,1024,128,8]{2,1,3,0:T(8,128)}, u32[]{:S(2)}) copy-start(f32[2,1024,128,8]{2,1,3,0:T(8,128)} %get-tuple-element.279) | copy-start | bytes 25165828
  195.5 4.5 %copy-start.12 = (f32[16]{0:T(128)S(1)}, f32[16]{0:T(128)}, u32[]{:S(2)}) copy-start(f32[16]{0:T(128)} %get-tuple-element.529) | copy-start | bytes 196 | tf_op jit(solution)/shard_map/while
  195.5 4.5 %copy-start.13 = (f32[16]{0:T(128)S(1)}, f32[16]{0:T(128)}, u32[]{:S(2)}) copy-start(f32[16]{0:T(128)} %get-tuple-element.531) | copy-start | bytes 196 | tf_op jit(solution)/shard_map/while
  195.5 4.7 %copy-start.10 = (f32[16]{0:T(128)S(1)}, f32[16]{0:T(128)}, u32[]{:S(2)}) copy-start(f32[16]{0:T(128)} %get-tuple-element.523) | copy-start | bytes 196 | tf_op jit(solution)/shard_map/while
  195.5 4.7 %copy-start.11 = (f32[16]{0:T(128)S(1)}, f32[16]{0:T(128)}, u32[]{:S(2)}) copy-start(f32[16]{0:T(128)} %get-tuple-element.525) | copy-start | bytes 196 | tf_op jit(solution)/shard_map/while
  195.5 4.9 %copy-start.8 = (f32[16]{0:T(128)S(1)}, f32[16]{0:T(128)}, u32[]{:S(2)}) copy-start(f32[16]{0:T(128)} %get-tuple-element.517) | copy-start | bytes 196 | tf_op jit(solution)/shard_map/while
  195.5 4.9 %copy-start.9 = (f32[16]{0:T(128)S(1)}, f32[16]{0:T(128)}, u32[]{:S(2)}) copy-start(f32[16]{0:T(128)} %get-tuple-element.519) | copy-start | bytes 196 | tf_op jit(solution)/shard_map/while
  195.5 5.0 %copy-start.7 = (f32[16]{0:T(128)S(1)}, f32[16]{0:T(128)}, u32[]{:S(2)}) copy-start(f32[16]{0:T(128)} %get-tuple-element.513) | copy-start | bytes 196 | tf_op jit(solution)/shard_map/while
  196.8 4.0 %copy-start.25 = (f32[16]{0:T(128)S(1)}, f32[16]{0:T(128)}, u32[]{:S(2)}) copy-start(f32[16]{0:T(128)} %get-tuple-element.504) | copy-start | bytes 196 | tf_op jit(solution)/shard_map/while
  196.8 4.0 %copy-start.26 = (f32[16]{0:T(128)S(1)}, f32[16]{0:T(128)}, u32[]{:S(2)}) copy-start(f32[16]{0:T(128)} %get-tuple-element.506) | copy-start | bytes 196 | tf_op jit(solution)/shard_map/while
  215.9 4.5 %copy-start.12 = (f32[16]{0:T(128)S(1)}, f32[16]{0:T(128)}, u32[]{:S(2)}) copy-start(f32[16]{0:T(128)} %get-tuple-element.529) | copy-start | bytes 196 | tf_op jit(solution)/shard_map/while
  215.9 4.5 %copy-start.13 = (f32[16]{0:T(128)S(1)}, f32[16]{0:T(128)}, u32[]{:S(2)}) copy-start(f32[16]{0:T(128)} %get-tuple-element.531) | copy-start | bytes 196 | tf_op jit(solution)/shard_map/while
  216.0 4.7 %copy-start.10 = (f32[16]{0:T(128)S(1)}, f32[16]{0:T(128)}, u32[]{:S(2)}) copy-start(f32[16]{0:T(128)} %get-tuple-element.523) | copy-start | bytes 196 | tf_op jit(solution)/shard_map/while
  216.0 4.7 %copy-start.11 = (f32[16]{0:T(128)S(1)}, f32[16]{0:T(128)}, u32[]{:S(2)}) copy-start(f32[16]{0:T(128)} %get-tuple-element.525) | copy-start | bytes 196 | tf_op jit(solution)/shard_map/while
  216.0 4.9 %copy-start.8 = (f32[16]{0:T(128)S(1)}, f32[16]{0:T(128)}, u32[]{:S(2)}) copy-start(f32[16]{0:T(128)} %get-tuple-element.517) | copy-start | bytes 196 | tf_op jit(solution)/shard_map/while
  216.0 4.9 %copy-start.9 = (f32[16]{0:T(128)S(1)}, f32[16]{0:T(128)}, u32[]{:S(2)}) copy-start(f32[16]{0:T(128)} %get-tuple-element.519) | copy-start | bytes 196 | tf_op jit(solution)/shard_map/while
  216.0 5.0 %copy-start.7 = (f32[16]{0:T(128)S(1)}, f32[16]{0:T(128)}, u32[]{:S(2)}) copy-start(f32[16]{0:T(128)} %get-tuple-element.513) | copy-start | bytes 196 | tf_op jit(solution)/shard_map/while
  217.2 4.0 %copy-start.25 = (f32[16]{0:T(128)S(1)}, f32[16]{0:T(128)}, u32[]{:S(2)}) copy-start(f32[16]{0:T(128)} %get-tuple-element.504) | copy-start | bytes 196 | tf_op jit(solution)/shard_map/while
  217.2 4.0 %copy-start.26 = (f32[16]{0:T(128)S(1)}, f32[16]{0:T(128)}, u32[]{:S(2)}) copy-start(f32[16]{0:T(128)} %get-tuple-element.506) | copy-start | bytes 196 | tf_op jit(solution)/shard_map/while
  236.4 4.5 %copy-start.12 = (f32[16]{0:T(128)S(1)}, f32[16]{0:T(128)}, u32[]{:S(2)}) copy-start(f32[16]{0:T(128)} %get-tuple-element.529) | copy-start | bytes 196 | tf_op jit(solution)/shard_map/while
  236.4 4.5 %copy-start.13 = (f32[16]{0:T(128)S(1)}, f32[16]{0:T(128)}, u32[]{:S(2)}) copy-start(f32[16]{0:T(128)} %get-tuple-element.531) | copy-start | bytes 196 | tf_op jit(solution)/shard_map/while
  236.4 4.7 %copy-start.10 = (f32[16]{0:T(128)S(1)}, f32[16]{0:T(128)}, u32[]{:S(2)}) copy-start(f32[16]{0:T(128)} %get-tuple-element.523) | copy-start | bytes 196 | tf_op jit(solution)/shard_map/while
  236.5 4.7 %copy-start.11 = (f32[16]{0:T(128)S(1)}, f32[16]{0:T(128)}, u32[]{:S(2)}) copy-start(f32[16]{0:T(128)} %get-tuple-element.525) | copy-start | bytes 196 | tf_op jit(solution)/shard_map/while
  236.5 4.9 %copy-start.8 = (f32[16]{0:T(128)S(1)}, f32[16]{0:T(128)}, u32[]{:S(2)}) copy-start(f32[16]{0:T(128)} %get-tuple-element.517) | copy-start | bytes 196 | tf_op jit(solution)/shard_map/while
  236.5 4.9 %copy-start.9 = (f32[16]{0:T(128)S(1)}, f32[16]{0:T(128)}, u32[]{:S(2)}) copy-start(f32[16]{0:T(128)} %get-tuple-element.519) | copy-start | bytes 196 | tf_op jit(solution)/shard_map/while
  236.5 5.0 %copy-start.7 = (f32[16]{0:T(128)S(1)}, f32[16]{0:T(128)}, u32[]{:S(2)}) copy-start(f32[16]{0:T(128)} %get-tuple-element.513) | copy-start | bytes 196 | tf_op jit(solution)/shard_map/while
  237.7 4.0 %copy-start.25 = (f32[16]{0:T(128)S(1)}, f32[16]{0:T(128)}, u32[]{:S(2)}) copy-start(f32[16]{0:T(128)} %get-tuple-element.504) | copy-start | bytes 196 | tf_op jit(solution)/shard_map/while
  237.7 4.0 %copy-start.26 = (f32[16]{0:T(128)S(1)}, f32[16]{0:T(128)}, u32[]{:S(2)}) copy-start(f32[16]{0:T(128)} %get-tuple-element.506) | copy-start | bytes 196 | tf_op jit(solution)/shard_map/while
  256.8 4.5 %copy-start.12 = (f32[16]{0:T(128)S(1)}, f32[16]{0:T(128)}, u32[]{:S(2)}) copy-start(f32[16]{0:T(128)} %get-tuple-element.529) | copy-start | bytes 196 | tf_op jit(solution)/shard_map/while
  256.9 4.5 %copy-start.13 = (f32[16]{0:T(128)S(1)}, f32[16]{0:T(128)}, u32[]{:S(2)}) copy-start(f32[16]{0:T(128)} %get-tuple-element.531) | copy-start | bytes 196 | tf_op jit(solution)/shard_map/while
  256.9 4.7 %copy-start.10 = (f32[16]{0:T(128)S(1)}, f32[16]{0:T(128)}, u32[]{:S(2)}) copy-start(f32[16]{0:T(128)} %get-tuple-element.523) | copy-start | bytes 196 | tf_op jit(solution)/shard_map/while
  256.9 4.7 %copy-start.11 = (f32[16]{0:T(128)S(1)}, f32[16]{0:T(128)}, u32[]{:S(2)}) copy-start(f32[16]{0:T(128)} %get-tuple-element.525) | copy-start | bytes 196 | tf_op jit(solution)/shard_map/while
  256.9 4.9 %copy-start.8 = (f32[16]{0:T(128)S(1)}, f32[16]{0:T(128)}, u32[]{:S(2)}) copy-start(f32[16]{0:T(128)} %get-tuple-element.517) | copy-start | bytes 196 | tf_op jit(solution)/shard_map/while
  256.9 4.9 %copy-start.9 = (f32[16]{0:T(128)S(1)}, f32[16]{0:T(128)}, u32[]{:S(2)}) copy-start(f32[16]{0:T(128)} %get-tuple-element.519) | copy-start | bytes 196 | tf_op jit(solution)/shard_map/while
  256.9 5.0 %copy-start.7 = (f32[16]{0:T(128)S(1)}, f32[16]{0:T(128)}, u32[]{:S(2)}) copy-start(f32[16]{0:T(128)} %get-tuple-element.513) | copy-start | bytes 196 | tf_op jit(solution)/shard_map/while
  258.1 4.0 %copy-start.25 = (f32[16]{0:T(128)S(1)}, f32[16]{0:T(128)}, u32[]{:S(2)}) copy-start(f32[16]{0:T(128)} %get-tuple-element.504) | copy-start | bytes 196 | tf_op jit(solution)/shard_map/while
  258.1 4.0 %copy-start.26 = (f32[16]{0:T(128)S(1)}, f32[16]{0:T(128)}, u32[]{:S(2)}) copy-start(f32[16]{0:T(128)} %get-tuple-element.506) | copy-start | bytes 196 | tf_op jit(solution)/shard_map/while
  265.0 4.0 %copy-start.1 = (bf16[128,1024]{1,0:T(8,128)(2,1)S(1)}, bf16[128,1024]{1,0:T(8,128)(2,1)}, u32[]{:S(2)}) copy-start(bf16[128,1024]{1,0:T(8,128)(2,1)} %param.23) | copy-start | bytes 786436
  (44 other events, 75.7 us)
Sparse Core Ops, SparseCore 0:
  91.5 41.4 all-gather.7
  135.2 40.2 all-gather.5
